TPU v7x, 256 devices: a whole 4x4x8 slice. The times are simulated.
256 devices in a mesh: cuts: 4 (over y), blk: 64 (over x, z, core).
Axes of the slice: x: 4, y: 4, z: 8, core: 2. Of those that a mesh axis runs over, the one named last changes fastest.
Arguments:
- gap_load: float32 [4, 128, 2, 256, 128], P('cuts', 'blk'), may hold values from -24 to 24
- offsets: int32 [4, 128, 2], P('cuts', 'blk'), may hold values from -1 to 255, as said below
- corner_map: int32 [4, 128, 4], P('cuts', 'blk'), may hold values from -1 to 511, as said below
- flexibility: float32 [4, 128, 1024, 1024], P('cuts', 'blk'), may hold values from -0.5 to 4.5, as said below
- coupling: float32 [4, 128, 12, 1024], P('cuts', 'blk'), may hold values from -1.25 to 1.25
- corner_rows: float32 [4, 128, 12, 1536], P('cuts', 'blk'), may hold values from -0.1 to 1.1, as said below
Outputs:
- multipliers: float32 [4, 128, 2, 256, 128], P('cuts', 'blk')
- residual: float32 [4, 128, 2, 256, 128], P('cuts', 'blk')
Inputs may be any that keep to these rules, and one draw needn't show every extreme that they name: `offsets`: on an interface owned by a subdomain, the neighbour's dof k matches the owner's dof (k + offset) mod 256; -1 marks an interface without multipliers: the tunnel's far end, or one that touches an excavated subdomain. `corner_map`: entries k = 0, 1, 2, 3 are the corners at near-left, near-right, far-left, far-right. Entry 2 of subdomain (r, c) is never -1, and every node is entry 2 of exactly one subdomain; the same node is entry 3 of (r, (c - 1) mod 128) and, for r + 1 < 4, entries 0 of (r + 1, c) and 1 of (r + 1, (c - 1) mod 128), and no other entry. -1 marks a clamped corner at the tunnel's near end. `flexibility`: each block is symmetric positive definite. `corner_rows`: row 3 k + j of a subdomain is row 3 m + j of one symmetric positive definite matrix of order 3 * 512, with m = corner_map entry k; zero rows where that entry is -1.
All inputs are finite; a program needn't handle non-finite values.
Results may differ from a plain program's by a relative error of at most 0.00021.
Values sent between devices are 32-bit elements; how exact they have to be, the bound alone decides.
A program may use at most 64 MiB of HBM per device.

v0:
```python
import jax
import jax.numpy as jnp
from jax import lax
from jax.sharding import PartitionSpec as P

ITERS = 3
HIGH = lax.Precision.HIGHEST


def from_behind(value, axis, steps):
    count = lax.axis_size(axis)
    first, last = (max(0, -steps), min(count, count - steps))
    return lax.ppermute(value, axis, [(source, source + steps) for source in range(first, last)])


def passed_along(value, axis, steps):
    count = lax.axis_size(axis)
    pairs = [(source, (source + steps) % count) for source in range(count)]
    return lax.ppermute(value, axis, pairs)


def rotate(values, amounts, orient):
    face_size = values.shape[-2]
    indices = (jnp.arange(face_size, dtype=jnp.int32) + orient * amounts[..., None]) % face_size
    return jnp.take_along_axis(values, indices[..., None], axis=-2)


def corner_indices(corner_map, dof_count):
    spread = 3 * corner_map[..., None] + jnp.arange(3, dtype=jnp.int32)
    spread = jnp.where(corner_map[..., None] >= 0, spread, dof_count)
    return spread.reshape(corner_map.shape[0], corner_map.shape[1], 12)


def inner_sum(first, second):
    return jnp.sum(first * second, axis=(0, 1, 2, 3))


def squares(residual):
    return lax.psum(inner_sum(residual, residual), ("cuts", "blk"))


def per_device(gap_load, offsets, corner_map, flexibility, coupling, corner_rows):
    cycle_count, circ_count, _, face_size, load_count = gap_load.shape
    dof_count = corner_rows.shape[-1]
    active = (offsets >= 0).astype(jnp.float32)[..., None, None]
    corner_dofs = corner_indices(corner_map, dof_count)
    residual = gap_load * active
    multipliers = jnp.zeros_like(residual)
    direction = residual
    norm_now = squares(residual)
    for iteration in range(ITERS):
        sent_far = -rotate(direction[:, :, 0], offsets[:, :, 0], 1)
        sent_right = -rotate(direction[:, :, 1], offsets[:, :, 1], 1)
        edge_near = from_behind(sent_far[-1], "cuts", 1)
        edge_left = passed_along(sent_right[:, -1], "blk", 1)
        nearside = jnp.concatenate([edge_near[None], sent_far[:-1]], axis=0)
        leftside = jnp.concatenate([edge_left[:, None], sent_right[:, :-1]], axis=1)
        loads = jnp.stack([nearside, direction[:, :, 0], leftside, direction[:, :, 1]], axis=2)
        loads = loads.reshape(cycle_count, circ_count, 4 * face_size, load_count)
        operator_corner_terms = jnp.einsum("rcki,rcin->rckn", coupling, loads, precision=HIGH)
        partial_value = jnp.zeros((dof_count, load_count), jnp.float32)
        partial_value = partial_value.at[corner_dofs.reshape(-1)].add(
            operator_corner_terms.reshape(-1, load_count), mode="drop"
        )
        coarse = lax.psum(partial_value, ("cuts", "blk"))
        corner_values = jnp.einsum("rckm,mn->rckn", corner_rows, coarse, precision=HIGH)
        moved = jnp.einsum("rcij,rcjn->rcin", flexibility, loads, precision=HIGH)
        moved = moved + jnp.einsum("rcki,rckn->rcin", coupling, corner_values, precision=HIGH)
        moved = moved.reshape(cycle_count, circ_count, 4, face_size, load_count)
        from_far = from_behind(moved[0, :, 0], "cuts", -1)
        from_right = passed_along(moved[:, 0, 2], "blk", -1)
        far_near = jnp.concatenate([moved[1:, :, 0], from_far[None]], axis=0)
        right_left = jnp.concatenate([moved[:, 1:, 2], from_right[:, None]], axis=1)
        jump_far = moved[:, :, 1] - rotate(far_near, offsets[:, :, 0], -1)
        jump_right = moved[:, :, 3] - rotate(right_left, offsets[:, :, 1], -1)
        mapped = jnp.stack([jump_far, jump_right], axis=2) * active
        step_size = norm_now / lax.psum(inner_sum(direction, mapped), ("cuts", "blk"))
        multipliers = multipliers + step_size * direction
        residual = residual - step_size * mapped
        norm_next = squares(residual)
        direction = residual + norm_next / norm_now * direction
        norm_now = norm_next
    return (multipliers, residual)


def solution(mesh):
    in_specs = (
        P("cuts", "blk", None, None, None),
        P("cuts", "blk", None),
        P("cuts", "blk", None),
        P("cuts", "blk", None, None),
        P("cuts", "blk", None, None),
        P("cuts", "blk", None, None),
    )
    out_specs = (P("cuts", "blk", None, None, None), P("cuts", "blk", None, None, None))
    return jax.shard_map(
        per_device, mesh=mesh, in_specs=in_specs, out_specs=out_specs, check_vma=False
    )
```

profile of v0, /device:TPU:1, one launch (start us, length us, event | category | flops | bytes accessed | tf_op | source)
XLA Modules:
  0.0 1306.6 jit_solution(7525697432891195552)
XLA Ops:
  8.0 1.0 multiply_reduce_fusion.7
  9.2 1.1 copy_multiply_fusion
  10.4 3.7 gather_fusion.1
  14.3 3.1 collective-permute-start.1
  17.6 3.7 gather_fusion
  21.4 3.2 collective-permute-start
  25.0 4.6 collective-permute-done
  30.7 1.0 convolution_bitcast_fusion.5
  31.7 1.6 scatter_custom_fusion
  33.4 11.0 fusion.4
  44.4 248.0 %all-reduce.5.cloned.1.call-done = f32[1536,128]{1,0:T(8,128)} async-done(((f32[1536,128]{1,0:T(8,128)}), f32[1536,128]{1,0:T(8,128)}) %all-reduce.5.cloned.1.call-update) | async-done | bytes 786448 | tf_op jit(solution)/shard_map/psum | solution.py:65
  292.4 1.8 convolution_bitcast_fusion.4
  294.2 2.0 fusion.8
  296.2 1.7 reshape.723
  298.3 2.4 collective-permute-start.3
  301.8 1.3 collective-permute-start.2
  303.1 3.7 gather_fusion.3
  306.9 2.0 collective-permute-done.2
  308.9 3.7 gather_fusion.2
  312.9 78.9 %all-reduce = (f32[128]{0:T(128)S(1)}, f32[128]{0:T(128)S(1)}) all-reduce(f32[128]{0:T(128)S(1)} %get-tuple-element.8, f32[128]{0:T(128)S(1)} %get-tuple-element.7), channel_id=1, replica_groups=mesh['cuts'=4,'blk'=64] {'cuts','blk'}, use_global_device_ids=true, to_apply=%region_1.2 | all-reduce | flops 256 | bytes 2048 | tf_op jit(solution)/shard_map/psum | solution.py:39
  392.0 72.6 %psum.66 = f32[128]{0:T(128)S(1)} all-reduce(f32[128]{0:T(128)S(1)} %multiply_reduce_fusion.3), channel_id=1, replica_groups=mesh['cuts'=4,'blk'=64] {'cuts','blk'}, use_global_device_ids=true, to_apply=%region_7.9 | all-reduce | flops 128 | bytes 1024 | tf_op jit(solution)/shard_map/psum | solution.py:39
  464.9 3.7 gather_fusion.4
  468.7 3.7 gather_fusion.5
  472.5 2.4 collective-permute-start.4
  475.0 2.7 collective-permute-start.5
  477.7 1.9 collective-permute-done.5
  481.0 1.0 convolution_bitcast_fusion.3
  482.0 1.6 scatter_custom_fusion.1
  483.9 11.0 fusion.2
  494.9 243.5 %all-reduce.7.cloned.1.call-done = f32[1536,128]{1,0:T(8,128)} async-done(((f32[1536,128]{1,0:T(8,128)}), f32[1536,128]{1,0:T(8,128)}) %all-reduce.7.cloned.1.call-update) | async-done | bytes 786448 | tf_op jit(solution)/shard_map/psum | solution.py:65
  738.4 1.7 convolution_bitcast_fusion.2
  740.1 2.0 fusion.7
  742.1 1.7 reshape.726
  744.9 2.2 collective-permute-start.7
  748.1 1.3 collective-permute-start.6
  750.5 3.7 gather_fusion.7
  755.2 3.7 gather_fusion.6
  759.9 80.2 %psum.68 = f32[128]{0:T(128)S(1)} all-reduce(f32[128]{0:T(128)S(1)} %multiply_reduce_fusion.2), channel_id=1, replica_groups=mesh['cuts'=4,'blk'=64] {'cuts','blk'}, use_global_device_ids=true, to_apply=%region_11.13 | all-reduce | flops 128 | bytes 1024 | tf_op jit(solution)/shard_map/psum | solution.py:77
  840.9 72.8 %psum.69 = f32[128]{0:T(128)S(1)} all-reduce(f32[128]{0:T(128)S(1)} %get-tuple-element.15), channel_id=1, replica_groups=mesh['cuts'=4,'blk'=64] {'cuts','blk'}, use_global_device_ids=true, to_apply=%region_13.15 | all-reduce | flops 128 | bytes 1024 | tf_op jit(solution)/shard_map/psum | solution.py:39
  915.3 3.7 gather_fusion.8
  919.8 3.7 gather_fusion.9
  923.6 2.2 collective-permute-start.8
  925.8 2.7 collective-permute-start.9
  928.5 1.9 collective-permute-done.9
  930.8 1.3 copy.59
  932.2 1.8 reshape.727
  934.0 1.0 convolution_bitcast_fusion.1
  935.0 1.7 scatter_custom_fusion.2
  936.7 12.0 fusion
  948.8 242.0 %all-reduce.9.cloned.1.call-done = f32[1536,128]{1,0:T(8,128)} async-done(((f32[1536,128]{1,0:T(8,128)}), f32[1536,128]{1,0:T(8,128)}) %all-reduce.9.cloned.1.call-update) | async-done | bytes 786448 | tf_op jit(solution)/shard_map/psum | solution.py:65
  1190.8 1.7 convolution_bitcast_fusion
  1192.5 3.3 fusion.6
  1195.8 1.7 reshape.729
  1198.5 1.7 copy.88
  1200.1 2.3 collective-permute-start.11
  1202.4 1.5 fusion.46
  1203.9 1.8 copy.85
  1205.7 1.8 copy.86
  1207.5 1.1 copy.84
  1208.6 1.3 collective-permute-start.10
  1210.8 3.7 gather_fusion.11
  1214.5 1.1 fusion.18
  1215.9 3.7 gather_fusion.10
  1220.0 77.9 %psum.71 = f32[128]{0:T(128)S(1)} all-reduce(f32[128]{0:T(128)S(1)} %multiply_reduce_fusion), channel_id=1, replica_groups=mesh['cuts'=4,'blk'=64] {'cuts','blk'}, use_global_device_ids=true, to_apply=%region_17.19 | all-reduce | flops 128 | bytes 1024 | tf_op jit(solution)/shard_map/psum | solution.py:77
  (129 shorter events, 21.0 us)
Async XLA Ops:
  7.2 285.2 %copy-start = (f32[1,2,12,1536]{3,1,2,0:T(2,128)S(1)}, f32[1,2,12,1536]{3,1,2,0:T(2,128)}, u32[]{:S(2)}) copy-start(f32[1,2,12,1536]{3,1,2,0:T(2,128)} %param.13) | copy-start | bytes 442372
  7.2 17.4 %copy-start.12 = (s32[1,2,4]{2,1,0:T(2,128)S(1)}, s32[1,2,4]{2,1,0:T(2,128)}, u32[]{:S(2)}) copy-start(s32[1,2,4]{2,1,0:T(2,128)} %param.10) | copy-start | bytes 100
  7.2 23.5 %copy-start.2 = (f32[1,2,12,1024]{3,1,2,0:T(2,128)S(1)}, f32[1,2,12,1024]{3,1,2,0:T(2,128)}, u32[]{:S(2)}) copy-start(f32[1,2,12,1024]{3,1,2,0:T(2,128)} %param.12) | copy-start | bytes 294916
  7.2 285.2 %all-reduce.5.cloned.1.call-start = ((), (), s32[]{:S(2)}) async-start(), calls=%async_computation | async-start | bytes 1572864 | tf_op jit(solution)/shard_map/psum | solution.py:65
  9.0 463.4 %copy-start.5 = (pred[2,256]{1,0:T(4,128)(4,1)}, pred[2,256]{1,0:T(4,128)(4,1)S(1)}, u32[]{:S(2)}) copy-start(pred[2,256]{1,0:T(4,128)(4,1)S(1)} %and_bitcast_fusion.2) | copy-start | bytes 1540
  14.3 10.7 collective-permute-start.1
  17.5 451.1 %copy-start.7 = (pred[2,256]{1,0:T(4,128)(4,1)}, pred[2,256]{1,0:T(4,128)(4,1)S(1)}, u32[]{:S(2)}) copy-start(pred[2,256]{1,0:T(4,128)(4,1)S(1)} %and_bitcast_fusion.3) | copy-start | bytes 1540
  21.4 8.3 collective-permute-start
  25.0 457.0 %copy-start.13 = (s32[24]{0:T(128)}, s32[24]{0:T(128)S(1)}, u32[]{:S(2)}) copy-start(s32[24]{0:T(128)S(1)} %fusion.45) | copy-start | bytes 292
  33.3 705.1 %all-reduce.7.cloned.1.call-start = ((), (), s32[]{:S(2)}) async-start(), calls=%async_computation.1 | async-start | bytes 1572864 | tf_op jit(solution)/shard_map/psum | solution.py:65
  292.4 20.3 %copy-start.1 = (f32[1,2,2,256,128]{4,3,2,1,0:T(8,128)S(1)}, f32[1,2,2,256,128]{4,3,2,1,0:T(8,128)}, u32[]{:S(2)}) copy-start(f32[1,2,2,256,128]{4,3,2,1,0:T(8,128)} %param.8) | copy-start | bytes 1572868
  298.3 4.8 collective-permute-start.3
  301.8 7.1 collective-permute-start.2
  464.6 16.3 %copy-start.14 = (f32[128]{0:T(128)}, f32[128]{0:T(128)S(1)}, u32[]{:S(2)}) copy-start(f32[128]{0:T(128)S(1)} %psum.66) | copy-start | bytes 1540
  464.6 16.3 %copy-start.8 = (f32[128]{0:T(128)}, f32[128]{0:T(128)S(1)}, u32[]{:S(2)}) copy-start(f32[128]{0:T(128)S(1)} %div.16) | copy-start | bytes 1540
  472.5 7.4 collective-permute-start.4
  475.0 4.6 collective-permute-start.5
  483.6 707.2 %all-reduce.9.cloned.1.call-start = ((), (), s32[]{:S(2)}) async-start(), calls=%async_computation.2 | async-start | bytes 1572864 | tf_op jit(solution)/shard_map/psum | solution.py:65
  744.9 4.7 collective-permute-start.7
  748.1 7.1 collective-permute-start.6
  755.2 168.2 %copy-start.6 = (pred[2,256]{1,0:T(4,128)(4,1)S(1)}, pred[2,256]{1,0:T(4,128)(4,1)}, u32[]{:S(2)}) copy-start(pred[2,256]{1,0:T(4,128)(4,1)} %copy-done.5) | copy-start | bytes 1540
  840.7 91.5 %copy-start.10 = (f32[128]{0:T(128)}, f32[128]{0:T(128)S(1)}, u32[]{:S(2)}) copy-start(f32[128]{0:T(128)S(1)} %div.17) | copy-start | bytes 1540
  840.9 73.4 %copy-start.3 = (f32[1,2,2,256,128]{4,3,1,2,0:T(8,128)}, f32[1,2,2,256,128]{4,3,1,2,0:T(8,128)S(1)}, u32[]{:S(2)}) copy-start(f32[1,2,2,256,128]{4,3,1,2,0:T(8,128)S(1)} %get-tuple-element.16) | copy-start | bytes 1572868
  913.7 20.2 %copy-start.15 = (f32[128]{0:T(128)}, f32[128]{0:T(128)S(1)}, u32[]{:S(2)}) copy-start(f32[128]{0:T(128)S(1)} %psum.69) | copy-start | bytes 1540
  923.6 7.2 collective-permute-start.8
  925.8 4.6 collective-permute-start.9
  1192.5 105.4 %copy-start.4 = (f32[1,2,2,256,128]{4,3,1,2,0:T(8,128)S(1)}, f32[1,2,2,256,128]{4,3,1,2,0:T(8,128)}, u32[]{:S(2)}) copy-start(f32[1,2,2,256,128]{4,3,1,2,0:T(8,128)} %copy-done.3) | copy-start | bytes 1572868
  1192.5 105.4 %copy-start.9 = (f32[128]{0:T(128)S(1)}, f32[128]{0:T(128)}, u32[]{:S(2)}) copy-start(f32[128]{0:T(128)} %copy-done.8) | copy-start | bytes 1540
  1192.5 105.4 %copy-start.11 = (f32[128]{0:T(128)S(1)}, f32[128]{0:T(128)}, u32[]{:S(2)}) copy-start(f32[128]{0:T(128)} %copy-done.10) | copy-start | bytes 1540
  1195.8 102.1 %copy-start.16 = (f32[128]{0:T(128)S(1)}, f32[128]{0:T(128)}, u32[]{:S(2)}) copy-start(f32[128]{0:T(128)} %copy-done.15) | copy-start | bytes 1540
  1200.1 9.8 collective-permute-start.11
  1208.6 7.3 collective-permute-start.10
Sparse Core Ops, SparseCore 0:
  33.4 258.9 all-reduce.4
  483.7 254.6 all-reduce.6
  936.8 253.8 all-reduce.8
where the time goes:
time: 1320 us; the launch traced here: 1310 us
  waiting for transfers between devices  746 us (57%)
  blocking collectives  382 us (29%)
  local copies, waits for them, and re-layouts  68.4 us (5%)
  matrix products  49.6 us (4%)
  starting transfers between devices  27.4 us (2%)
  other arithmetic  18.2 us (1%)
  between operations  14.7 us (1%)
    psum x3, waiting for transfers between devices, per_device(): coarse = lax.psum(partial_value, ('cuts', 'blk'))  733 us
    psum x3, blocking collectives, squares(): return lax.psum(inner_sum(residual, residual), ('cuts', 'blk'))  224 us
    psum x2, blocking collectives, per_device(): lax.psum(inner_sum(direction, mapped), ('cuts', 'blk'))  158 us
    gather x12, local copies, waits for them, and re-layouts, rotate(): return jnp.take_along_axis(values, indices[..., None], axis=-2)  43.9 us
    dot_general x3, matrix products, per_device(): moved = jnp.einsum('rcij,rcjn->rcin', flexibility, loads, precision=HIGH)  34.1 us
  transfers between devices with their start and end apart: 15, of which 12 were waited for; matrix products, arithmetic and copies ran while one was open for 5% of the time, Pallas kernels for 0%

commit v1 on v0

--- a/solution.py
+++ b/solution.py
@@ -2,6 +2,7 @@
 import jax.numpy as jnp
 from jax import lax
 from jax.sharding import PartitionSpec as P
+from jax.lax import psum
 
 ITERS = 3
 HIGH = lax.Precision.HIGHEST
@@ -62,7 +63,7 @@
         partial_value = partial_value.at[corner_dofs.reshape(-1)].add(
             operator_corner_terms.reshape(-1, load_count), mode="drop"
         )
-        coarse = lax.psum(partial_value, ("cuts", "blk"))
+        coarse = psum(psum(partial_value, axis_name="cuts"), axis_name="blk")
         corner_values = jnp.einsum("rckm,mn->rckn", corner_rows, coarse, precision=HIGH)
         moved = jnp.einsum("rcij,rcjn->rcin", flexibility, loads, precision=HIGH)
         moved = moved + jnp.einsum("rcki,rckn->rcin", coupling, corner_values, precision=HIGH)

time: 1320 us -> 1260 us (0.955)
  waiting for transfers between devices: 746 us -> 691 us
    psum x3 -> x6, waiting for transfers between devices: 733 us -> 678 us  [per_device(): coarse = psum(psum(partial_value, axis_name='cuts'), axis_name='blk')]
  transfers between devices with their start and end apart: 15 -> 18, of which waited for: 12 -> 15; matrix products, arithmetic and copies ran while one was open for 5% -> 5% of each run, Pallas kernels for 0% -> 0%
where the time goes in v1:
time: 1260 us; the launch traced here: 1250 us
  waiting for transfers between devices  691 us (55%)
  blocking collectives  382 us (30%)
  local copies, waits for them, and re-layouts  68.4 us (5%)
  matrix products  49.6 us (4%)
  starting transfers between devices  27.6 us (2%)
  other arithmetic  18 us (1%)
  between operations  15.1 us (1%)
    psum x6, waiting for transfers between devices, per_device(): coarse = psum(psum(partial_value, axis_name='cuts'), axis_name='blk')  678 us
    psum x3, blocking collectives, squares(): return lax.psum(inner_sum(residual, residual), ('cuts', 'blk'))  224 us
    psum x2, blocking collectives, per_device(): lax.psum(inner_sum(direction, mapped), ('cuts', 'blk'))  158 us
    gather x12, local copies, waits for them, and re-layouts, rotate(): return jnp.take_along_axis(values, indices[..., None], axis=-2)  43.9 us
    dot_general x3, matrix products, per_device(): moved = jnp.einsum('rcij,rcjn->rcin', flexibility, loads, precision=HIGH)  34.1 us
  transfers between devices with their start and end apart: 18, of which 15 were waited for; matrix products, arithmetic and copies ran while one was open for 5% of the time, Pallas kernels for 0%

profile of v1, /device:TPU:1, one launch (start us, length us, event | category | flops | bytes accessed | tf_op | source)
XLA Modules:
  0.0 1252.1 jit_solution(6547937003601236646)
XLA Ops:
  9.2 1.1 copy_multiply_fusion
  10.4 3.7 gather_fusion.1
  14.3 3.1 collective-permute-start.1
  17.6 3.7 gather_fusion
  21.4 3.2 collective-permute-start
  24.8 4.8 collective-permute-done
  30.7 1.0 convolution_bitcast_fusion.5
  31.7 1.6 scatter_custom_fusion
  33.6 51.0 %all-reduce.8.cloned.1.call-done = f32[1536,128]{1,0:T(8,128)} async-done(((f32[1536,128]{1,0:T(8,128)}), f32[1536,128]{1,0:T(8,128)}) %all-reduce.8.cloned.1.call-update) | async-done | bytes 786448 | tf_op jit(solution)/shard_map/psum | solution.py:66
  84.6 11.0 fusion.4
  95.7 179.0 %all-reduce.10.cloned.1.call-done = f32[1536,128]{1,0:T(8,128)} async-done(((f32[1536,128]{1,0:T(8,128)}), f32[1536,128]{1,0:T(8,128)}) %all-reduce.10.cloned.1.call-update) | async-done | bytes 786448 | tf_op jit(solution)/shard_map/psum | solution.py:66
  274.7 1.8 convolution_bitcast_fusion.4
  276.4 2.0 fusion.8
  278.5 1.7 reshape.723
  280.5 2.5 collective-permute-start.3
  284.1 1.3 collective-permute-start.2
  285.5 3.7 gather_fusion.3
  289.3 2.0 collective-permute-done.2
  291.2 3.7 gather_fusion.2
  295.3 78.9 %all-reduce = (f32[128]{0:T(128)S(1)}, f32[128]{0:T(128)S(1)}) all-reduce(f32[128]{0:T(128)S(1)} %get-tuple-element.8, f32[128]{0:T(128)S(1)} %get-tuple-element.7), channel_id=1, replica_groups=mesh['cuts'=4,'blk'=64] {'cuts','blk'}, use_global_device_ids=true, to_apply=%region_1.2 | all-reduce | flops 256 | bytes 2048 | tf_op jit(solution)/shard_map/psum | solution.py:40
  374.4 72.4 %psum.88 = f32[128]{0:T(128)S(1)} all-reduce(f32[128]{0:T(128)S(1)} %multiply_reduce_fusion.3), channel_id=1, replica_groups=mesh['cuts'=4,'blk'=64] {'cuts','blk'}, use_global_device_ids=true, to_apply=%region_8.10 | all-reduce | flops 128 | bytes 1024 | tf_op jit(solution)/shard_map/psum | solution.py:40
  447.1 3.7 gather_fusion.4
  450.9 3.7 gather_fusion.5
  454.7 2.2 collective-permute-start.4
  457.0 2.7 collective-permute-start.5
  459.6 1.9 collective-permute-done.5
  464.0 1.6 scatter_custom_fusion.1
  465.6 46.1 %all-reduce.12.cloned.1.call-done = f32[1536,128]{1,0:T(8,128)} async-done(((f32[1536,128]{1,0:T(8,128)}), f32[1536,128]{1,0:T(8,128)}) %all-reduce.12.cloned.1.call-update) | async-done | bytes 786448 | tf_op jit(solution)/shard_map/psum | solution.py:66
  512.0 11.0 fusion.2
  523.0 178.7 %all-reduce.14.cloned.1.call-done = f32[1536,128]{1,0:T(8,128)} async-done(((f32[1536,128]{1,0:T(8,128)}), f32[1536,128]{1,0:T(8,128)}) %all-reduce.14.cloned.1.call-update) | async-done | bytes 786448 | tf_op jit(solution)/shard_map/psum | solution.py:66
  701.7 1.7 convolution_bitcast_fusion.2
  703.4 2.0 fusion.7
  705.4 1.7 reshape.726
  708.1 2.3 collective-permute-start.7
  711.5 1.3 collective-permute-start.6
  713.8 3.7 gather_fusion.7
  718.6 3.7 gather_fusion.6
  723.2 80.2 %psum.91 = f32[128]{0:T(128)S(1)} all-reduce(f32[128]{0:T(128)S(1)} %multiply_reduce_fusion.2), channel_id=1, replica_groups=mesh['cuts'=4,'blk'=64] {'cuts','blk'}, use_global_device_ids=true, to_apply=%region_13.15 | all-reduce | flops 128 | bytes 1024 | tf_op jit(solution)/shard_map/psum | solution.py:78
  804.3 72.8 %psum.92 = f32[128]{0:T(128)S(1)} all-reduce(f32[128]{0:T(128)S(1)} %get-tuple-element.15), channel_id=1, replica_groups=mesh['cuts'=4,'blk'=64] {'cuts','blk'}, use_global_device_ids=true, to_apply=%region_15.17 | all-reduce | flops 128 | bytes 1024 | tf_op jit(solution)/shard_map/psum | solution.py:40
  878.6 3.7 gather_fusion.8
  883.1 3.7 gather_fusion.9
  886.9 2.2 collective-permute-start.8
  889.2 2.7 collective-permute-start.9
  891.8 1.9 collective-permute-done.9
  894.2 1.3 copy.59
  895.5 1.8 reshape.727
  898.3 1.7 scatter_custom_fusion.2
  900.0 46.0 %all-reduce.16.cloned.1.call-done = f32[1536,128]{1,0:T(8,128)} async-done(((f32[1536,128]{1,0:T(8,128)}), f32[1536,128]{1,0:T(8,128)}) %all-reduce.16.cloned.1.call-update) | async-done | bytes 786448 | tf_op jit(solution)/shard_map/psum | solution.py:66
  946.1 12.0 fusion
  958.1 177.7 %all-reduce.18.cloned.1.call-done = f32[1536,128]{1,0:T(8,128)} async-done(((f32[1536,128]{1,0:T(8,128)}), f32[1536,128]{1,0:T(8,128)}) %all-reduce.18.cloned.1.call-update) | async-done | bytes 786448 | tf_op jit(solution)/shard_map/psum | solution.py:66
  1135.8 1.7 convolution_bitcast_fusion
  1137.5 3.3 fusion.6
  1140.8 1.7 reshape.729
  1143.5 1.7 copy.88
  1145.1 2.4 collective-permute-start.11
  1147.6 1.5 fusion.46
  1149.0 1.8 copy.85
  1150.9 1.8 copy.86
  1152.7 1.1 copy.84
  1153.8 1.3 collective-permute-start.10
  1156.0 3.7 gather_fusion.11
  1159.7 1.1 fusion.18
  1161.1 3.7 gather_fusion.10
  1165.1 77.9 %psum.95 = f32[128]{0:T(128)S(1)} all-reduce(f32[128]{0:T(128)S(1)} %multiply_reduce_fusion), channel_id=1, replica_groups=mesh['cuts'=4,'blk'=64] {'cuts','blk'}, use_global_device_ids=true, to_apply=%region_20.22 | all-reduce | flops 128 | bytes 1024 | tf_op jit(solution)/shard_map/psum | solution.py:78
  (138 shorter events, 24.0 us)
Async XLA Ops:
  7.2 267.5 %copy-start = (f32[1,2,12,1536]{3,1,2,0:T(2,128)S(1)}, f32[1,2,12,1536]{3,1,2,0:T(2,128)}, u32[]{:S(2)}) copy-start(f32[1,2,12,1536]{3,1,2,0:T(2,128)} %param.13) | copy-start | bytes 442372
  7.2 17.4 %copy-start.12 = (s32[1,2,4]{2,1,0:T(2,128)S(1)}, s32[1,2,4]{2,1,0:T(2,128)}, u32[]{:S(2)}) copy-start(s32[1,2,4]{2,1,0:T(2,128)} %param.10) | copy-start | bytes 100
  7.2 23.5 %copy-start.2 = (f32[1,2,12,1024]{3,1,2,0:T(2,128)S(1)}, f32[1,2,12,1024]{3,1,2,0:T(2,128)}, u32[]{:S(2)}) copy-start(f32[1,2,12,1024]{3,1,2,0:T(2,128)} %param.12) | copy-start | bytes 294916
  7.2 77.4 %all-reduce.8.cloned.1.call-start = ((), (), s32[]{:S(2)}) async-start(), calls=%async_computation | async-start | bytes 1572864 | tf_op jit(solution)/shard_map/psum | solution.py:66
  9.0 445.5 %copy-start.5 = (pred[2,256]{1,0:T(4,128)(4,1)}, pred[2,256]{1,0:T(4,128)(4,1)S(1)}, u32[]{:S(2)}) copy-start(pred[2,256]{1,0:T(4,128)(4,1)S(1)} %and_bitcast_fusion.2) | copy-start | bytes 1540
  14.3 10.5 collective-permute-start.1
  17.5 433.3 %copy-start.7 = (pred[2,256]{1,0:T(4,128)(4,1)}, pred[2,256]{1,0:T(4,128)(4,1)S(1)}, u32[]{:S(2)}) copy-start(pred[2,256]{1,0:T(4,128)(4,1)S(1)} %and_bitcast_fusion.3) | copy-start | bytes 1540
  21.4 8.3 collective-permute-start
  24.8 439.2 %copy-start.13 = (s32[24]{0:T(128)}, s32[24]{0:T(128)S(1)}, u32[]{:S(2)}) copy-start(s32[24]{0:T(128)S(1)} %fusion.45) | copy-start | bytes 292
  33.3 241.4 %all-reduce.10.cloned.1.call-start = ((), (), s32[]{:S(2)}) async-start(), calls=%async_computation.1 | async-start | bytes 1572864 | tf_op jit(solution)/shard_map/psum | solution.py:66
  84.6 427.1 %all-reduce.12.cloned.1.call-start = ((), (), s32[]{:S(2)}) async-start(), calls=%async_computation.2 | async-start | bytes 1572864 | tf_op jit(solution)/shard_map/psum | solution.py:66
  274.7 20.4 %copy-start.1 = (f32[1,2,2,256,128]{4,3,2,1,0:T(8,128)S(1)}, f32[1,2,2,256,128]{4,3,2,1,0:T(8,128)}, u32[]{:S(2)}) copy-start(f32[1,2,2,256,128]{4,3,2,1,0:T(8,128)} %param.8) | copy-start | bytes 1572868
  280.5 4.9 collective-permute-start.3
  284.1 7.1 collective-permute-start.2
  446.8 16.1 %copy-start.14 = (f32[128]{0:T(128)}, f32[128]{0:T(128)S(1)}, u32[]{:S(2)}) copy-start(f32[128]{0:T(128)S(1)} %psum.88) | copy-start | bytes 1540
  446.8 16.1 %copy-start.8 = (f32[128]{0:T(128)}, f32[128]{0:T(128)S(1)}, u32[]{:S(2)}) copy-start(f32[128]{0:T(128)S(1)} %div.16) | copy-start | bytes 1540
  454.7 7.2 collective-permute-start.4
  457.0 4.6 collective-permute-start.5
  465.6 236.1 %all-reduce.14.cloned.1.call-start = ((), (), s32[]{:S(2)}) async-start(), calls=%async_computation.3 | async-start | bytes 1572864 | tf_op jit(solution)/shard_map/psum | solution.py:66
  511.7 434.4 %all-reduce.16.cloned.1.call-start = ((), (), s32[]{:S(2)}) async-start(), calls=%async_computation.4 | async-start | bytes 1572864 | tf_op jit(solution)/shard_map/psum | solution.py:66
  708.1 4.7 collective-permute-start.7
  711.5 7.1 collective-permute-start.6
  718.6 168.2 %copy-start.6 = (pred[2,256]{1,0:T(4,128)(4,1)S(1)}, pred[2,256]{1,0:T(4,128)(4,1)}, u32[]{:S(2)}) copy-start(pred[2,256]{1,0:T(4,128)(4,1)} %copy-done.5) | copy-start | bytes 1540
  804.0 91.4 %copy-start.10 = (f32[128]{0:T(128)}, f32[128]{0:T(128)S(1)}, u32[]{:S(2)}) copy-start(f32[128]{0:T(128)S(1)} %div.17) | copy-start | bytes 1540
  804.3 73.4 %copy-start.3 = (f32[1,2,2,256,128]{4,3,1,2,0:T(8,128)}, f32[1,2,2,256,128]{4,3,1,2,0:T(8,128)S(1)}, u32[]{:S(2)}) copy-start(f32[1,2,2,256,128]{4,3,1,2,0:T(8,128)S(1)} %get-tuple-element.16) | copy-start | bytes 1572868
  877.1 20.2 %copy-start.15 = (f32[128]{0:T(128)}, f32[128]{0:T(128)S(1)}, u32[]{:S(2)}) copy-start(f32[128]{0:T(128)S(1)} %psum.92) | copy-start | bytes 1540
  886.9 7.2 collective-permute-start.8
  889.2 4.6 collective-permute-start.9
  900.0 235.8 %all-reduce.18.cloned.1.call-start = ((), (), s32[]{:S(2)}) async-start(), calls=%async_computation.5 | async-start | bytes 1572864 | tf_op jit(solution)/shard_map/psum | solution.py:66
  1137.5 105.6 %copy-start.4 = (f32[1,2,2,256,128]{4,3,1,2,0:T(8,128)S(1)}, f32[1,2,2,256,128]{4,3,1,2,0:T(8,128)}, u32[]{:S(2)}) copy-start(f32[1,2,2,256,128]{4,3,1,2,0:T(8,128)} %copy-done.3) | copy-start | bytes 1572868
  1137.5 105.6 %copy-start.9 = (f32[128]{0:T(128)S(1)}, f32[128]{0:T(128)}, u32[]{:S(2)}) copy-start(f32[128]{0:T(128)} %copy-done.8) | copy-start | bytes 1540
  1137.5 105.6 %copy-start.11 = (f32[128]{0:T(128)S(1)}, f32[128]{0:T(128)}, u32[]{:S(2)}) copy-start(f32[128]{0:T(128)} %copy-done.10) | copy-start | bytes 1540
  1140.8 102.2 %copy-start.16 = (f32[128]{0:T(128)S(1)}, f32[128]{0:T(128)}, u32[]{:S(2)}) copy-start(f32[128]{0:T(128)} %copy-done.15) | copy-start | bytes 1540
  1145.1 9.9 collective-permute-start.11
  1153.8 7.3 collective-permute-start.10
Sparse Core Ops, SparseCore 0:
  33.4 51.0 all-reduce.7
  88.0 186.6 all-reduce.9
  465.7 45.9 all-reduce.11
  515.0 186.6 all-reduce.13
  900.1 45.9 all-reduce.15
  949.4 186.4 all-reduce.17
